TPU v7x, 32 devices: a whole 2x2x4 slice. The times are simulated.
32 devices in a mesh: row: 8 (over z, y), col: 4 (over x, core).
Axes of the slice: x: 2, y: 2, z: 4, core: 2. Of those that a mesh axis runs over, the one named last changes fastest.
Arguments:
- leaf_inverse: bfloat16 [32, 1024, 1024], P(('row', 'col')), as said below
- leaf_rhs: bfloat16 [32, 1024, 512], P(('row', 'col')), may hold values from -6 to 6
- leaf_tiles: bfloat16 [32, 1024, 1024], P(('row', 'col')), may hold values from -0.09375 to 0.09375
- mid_inverse_t: bfloat16 [8, 1024, 1024], P('col', None, 'row'), as said below
- mid_rhs: bfloat16 [8, 1024, 512], P('col', 'row'), may hold values from -6 to 6
- mid_tiles: bfloat16 [8, 1024, 1024], P('col', None, 'row'), may hold values from -0.125 to 0.125
- top_inverse_t: bfloat16 [2, 1024, 1024], P(None, None, 'col'), as said below
- top_rhs: bfloat16 [2, 1024, 512], P(None, 'col'), may hold values from -6 to 6
- tile_lists: int32 [32, 1], P(('row', 'col')), may hold values from 0 to 1
Outputs:
- leaf_solved: bfloat16 [32, 1024, 512], P(('row', 'col'))
- mid_solved: bfloat16 [8, 1024, 512], P('col', 'row')
- top_solved: bfloat16 [2, 1024, 512], P(None, 'col')
Inputs may be any that keep to these rules, and one draw needn't show every extreme that they name: Each leaf_inverse[d] is zero above its diagonal and has diagonal entries between 0.75 and 1.25. Each mid_inverse_t[q] is zero below its diagonal and has diagonal entries between 0.75 and 1.25. Each top_inverse_t[b] is zero below its diagonal and has diagonal entries between 0.75 and 1.25.
All inputs are finite; a program needn't handle non-finite values.
Results may differ from a plain program's by a relative error of at most 0.0065.
Values may be sent and summed in bfloat16 or wider, within the bound.
No kernel may reach another device: no remote copies, remote signals or barrier semaphores. Data moves between devices by JAX's collectives and lax.ppermute only.
A program may use at most 64 MiB of HBM per device.

v0:
```python
import jax
import jax.numpy as jnp
from jax import lax
from jax.sharding import PartitionSpec as P

NB = 2


def solve_piece(inverse_cols, piece):
    return lax.dot_general(
        inverse_cols, piece, (((1,), (1,)), ((0,), (0,))), preferred_element_type=jnp.float32
    )


def local(
    leaf_inverse,
    leaf_rhs,
    leaf_tiles,
    mid_inverse_t,
    mid_rhs,
    mid_tiles,
    top_inverse_t,
    top_rhs,
    tile_lists,
):
    slot_ids = jnp.arange(NB, dtype=jnp.int32)[:, None, None]
    solved_leaf = jnp.dot(leaf_inverse[0], leaf_rhs[0], preferred_element_type=jnp.float32).astype(
        jnp.bfloat16
    )
    leaf_update = jnp.dot(leaf_tiles[0], solved_leaf, preferred_element_type=jnp.float32)
    mid_terms = jnp.where(slot_ids == tile_lists[0, 0], leaf_update[None], 0.0)
    mid_share = lax.psum_scatter(mid_terms, "row", scatter_dimension=1, tiled=True)
    mid_resid = (mid_rhs.astype(jnp.float32) - mid_share).astype(jnp.bfloat16)
    mid_own = solve_piece(
        mid_inverse_t, lax.all_gather(mid_resid, "row", axis=1, tiled=True)
    ).astype(jnp.bfloat16)
    top_terms = lax.dot_general(
        mid_tiles, mid_own, (((2,), (1,)), ((0,), (0,))), preferred_element_type=jnp.float32
    )
    summed_rows = lax.psum(top_terms, "row")
    top_share = lax.psum_scatter(summed_rows, "col", scatter_dimension=1, tiled=True)
    top_resid = (top_rhs.astype(jnp.float32) - top_share).astype(jnp.bfloat16)
    top_own = solve_piece(
        top_inverse_t, lax.all_gather(top_resid, "col", axis=1, tiled=True)
    ).astype(jnp.bfloat16)
    return (solved_leaf[None], mid_own, top_own)


def solution(mesh):
    placed = (
        P(("row", "col"), None, None),
        P(("row", "col"), None, None),
        P(("row", "col"), None, None),
        P("col", None, "row"),
        P("col", "row", None),
        P("col", None, "row"),
        P(None, None, "col"),
        P(None, "col", None),
        P(("row", "col"), None),
    )
    return jax.shard_map(
        local,
        mesh=mesh,
        in_specs=placed,
        out_specs=(P(("row", "col"), None, None), P("col", "row", None), P(None, "col", None)),
        check_vma=False,
    )
```

profile of v0, /device:TPU:0, one launch (start us, length us, event | category | flops | bytes accessed | tf_op | source)
XLA Modules:
  0.0 324.7 jit_solution(155862839401762226)
XLA Ops:
  7.2 0.0 copy-start
  7.2 0.0 reduce-scatter.3.cloned.1.call-start
  8.0 0.8 copy-done
  8.8 0.0 copy-start.4
  8.8 2.6 fusion.7
  11.4 0.0 copy-start.5
  11.4 1.0 copy-done.5
  12.4 0.0 copy-done.4
  12.4 1.3 fusion.4
  13.7 2.5 broadcast_select_fusion
  16.2 0.0 copy-start.3
  16.2 0.0 reduce-scatter.3.cloned.1.call-update
  16.2 0.0 all-gather.3.cloned.1.call-start
  16.3 0.9 copy-done.3
  17.2 0.2 copy.12
  17.3 0.0 copy-start.1
  17.4 90.4 %reduce-scatter.3.cloned.1.call-done = f32[2,128,512]{1,2,0:T(8,128)} async-done(((f32[2,1024,512]{1,2,0:T(8,128)}), f32[2,128,512]{1,2,0:T(8,128)}) %reduce-scatter.3.cloned.1.call-update) | async-done | bytes 524304 | tf_op jit(solution)/shard_map/reduce_scatter | solution.py:32
  107.8 1.8 subtract_convert_fusion.1
  109.6 0.0 all-gather.3.cloned.1.call-update
  109.6 0.0 reduce-scatter.5.cloned.1.call-start
  109.7 50.8 %all-gather.3.cloned.1.call-done = bf16[2,1024,512]{1,2,0:T(8,128)(2,1)} async-done(((bf16[2,128,512]{1,2,0:T(8,128)(2,1)}), bf16[2,1024,512]{1,2,0:T(8,128)(2,1)}) %all-gather.3.cloned.1.call-update) | async-done | bytes 2097168 | tf_op jit(solution)/shard_map/all_gather | solution.py:35
  160.4 2.4 convolution_convert_fusion.1
  162.8 0.0 copy-done.1
  162.8 2.7 convolution_bitcast_fusion
  165.5 0.0 copy-start.2
  165.5 0.0 reduce-scatter.5.cloned.1.call-update
  165.5 0.0 all-reduce.2.cloned.1.call-start
  165.5 42.7 %reduce-scatter.5.cloned.1.call-done = f32[2,256,512]{1,2,0:T(8,128)} async-done(((f32[2,1024,512]{1,2,0:T(8,128)}), f32[2,256,512]{1,2,0:T(8,128)}) %reduce-scatter.5.cloned.1.call-update) | async-done | bytes 1048592 | tf_op jit(solution)/shard_map/reduce_scatter | solution.py:41
  208.2 0.0 all-reduce.2.cloned.1.call-update
  208.3 0.0 all-gather.5.cloned.1.call-start
  208.3 0.0 copy-done.2
  208.3 0.2 copy.13
  208.5 81.3 %all-reduce.2.cloned.1.call-done = f32[2,256,512]{1,2,0:T(8,128)} async-done(((f32[2,256,512]{1,2,0:T(8,128)}), f32[2,256,512]{1,2,0:T(8,128)}) %all-reduce.2.cloned.1.call-update) | async-done | bytes 1048592 | tf_op jit(solution)/shard_map/psum | solution.py:40
  289.8 2.1 subtract_convert_fusion
  292.0 0.0 all-gather.5.cloned.1.call-update
  292.0 0.9 copy.14
  292.8 21.7 %all-gather.5.cloned.1.call-done = bf16[2,1024,512]{1,2,0:T(8,128)(2,1)} async-done(((bf16[2,256,512]{1,2,0:T(8,128)(2,1)}), bf16[2,1024,512]{1,2,0:T(8,128)(2,1)}) %all-gather.5.cloned.1.call-update) | async-done | bytes 2097168 | tf_op jit(solution)/shard_map/all_gather | solution.py:44
  314.6 2.6 fusion.10
  317.1 1.0 copy.15
  (1 shorter events, 0.0 us)
Async XLA Ops:
  7.2 1.6 copy-start
  7.2 100.6 %reduce-scatter.3.cloned.1.call-start = ((), (), s32[]{:S(2)}) async-start(), calls=%async_computation.2 | async-start | bytes 4718592 | tf_op jit(solution)/shard_map/reduce_scatter | solution.py:32
  8.8 3.6 %copy-start.4 = (bf16[1,1024,1024]{2,1,0:T(8,128)(2,1)S(1)}, bf16[1,1024,1024]{2,1,0:T(8,128)(2,1)}, u32[]{:S(2)}) copy-start(bf16[1,1024,1024]{2,1,0:T(8,128)(2,1)} %param.11) | copy-start | bytes 6291460
  11.4 1.0 copy-start.5
  16.2 0.9 copy-start.3
  16.2 144.2 %all-gather.3.cloned.1.call-start = ((), (), s32[]{:S(2)}) async-start(), calls=%async_computation.3 | async-start | bytes 2359296 | tf_op jit(solution)/shard_map/all_gather | solution.py:35
  17.3 145.5 %copy-start.1 = (bf16[2,1024,128]{2,1,0:T(8,128)(2,1)S(1)}, bf16[2,1024,128]{2,1,0:T(8,128)(2,1)}, u32[]{:S(2)}) copy-start(bf16[2,1024,128]{2,1,0:T(8,128)(2,1)} %param.14) | copy-start | bytes 1572868
  109.6 98.6 %reduce-scatter.5.cloned.1.call-start = ((), (), s32[]{:S(2)}) async-start(), calls=%async_computation.5 | async-start | bytes 5242880 | tf_op jit(solution)/shard_map/reduce_scatter | solution.py:41
  165.5 42.8 %copy-start.2 = (bf16[2,256,512]{2,1,0:T(8,128)(2,1)S(1)}, bf16[2,256,512]{2,1,0:T(8,128)(2,1)}, u32[]{:S(2)}) copy-start(bf16[2,256,512]{2,1,0:T(8,128)(2,1)} %param.16) | copy-start | bytes 1572868
  165.5 124.3 %all-reduce.2.cloned.1.call-start = ((), (), s32[]{:S(2)}) async-start(), calls=%async_computation.6 | async-start | bytes 2097152 | tf_op jit(solution)/shard_map/psum | solution.py:40
  208.3 106.3 %all-gather.5.cloned.1.call-start = ((), (), s32[]{:S(2)}) async-start(), calls=%async_computation.4 | async-start | bytes 2621440 | tf_op jit(solution)/shard_map/all_gather | solution.py:44
Sparse Core Ops, SparseCore 0:
  16.4 91.3 reduce-scatter.2
  110.4 49.9 all-gather.2
  165.6 42.5 reduce-scatter.4
  211.6 78.1 all-reduce.1
  292.1 22.3 all-gather.4
where the time goes:
time: 325 us
  waiting for transfers between devices  287 us (88%)
  between operations  14.6 us (4%)
  matrix products  11.5 us (4%)
  other arithmetic  6.48 us (2%)
  local copies, waits for them, and re-layouts  4.84 us (1%)
    reduce_scatter x1, waiting for transfers between devices, local(): lax.psum_scatter(mid_terms, 'row', scatter_dimension=1, tiled=True)  90.4 us
    psum x1, waiting for transfers between devices, local(): summed_rows = lax.psum(top_terms, 'row')  81.3 us
    all_gather x1, waiting for transfers between devices, local(): lax.all_gather(mid_resid, 'row', axis=1, tiled=True)  50.8 us
    reduce_scatter x1, waiting for transfers between devices, local(): lax.psum_scatter(summed_rows, 'col', scatter_dimension=1, tiled=True)  42.7 us
    all_gather x1, waiting for transfers between devices, local(): lax.all_gather(top_resid, 'col', axis=1, tiled=True)  21.7 us
  transfers between devices with their start and end apart: 5, of which 5 were waited for; matrix products, arithmetic and copies ran while one was open for 0% of the time, Pallas kernels for 0%

commit v1 on v0

--- a/solution.py
+++ b/solution.py
@@ -2,6 +2,7 @@
 import jax.numpy as jnp
 from jax import lax
 from jax.sharding import PartitionSpec as P
+from jax.lax import all_gather
 
 NB = 2
 
@@ -37,7 +38,7 @@
     top_terms = lax.dot_general(
         mid_tiles, mid_own, (((2,), (1,)), ((0,), (0,))), preferred_element_type=jnp.float32
     )
-    summed_rows = lax.psum(top_terms, "row")
+    summed_rows = jnp.sum(all_gather(top_terms, "row"), 0)
     top_share = lax.psum_scatter(summed_rows, "col", scatter_dimension=1, tiled=True)
     top_resid = (top_rhs.astype(jnp.float32) - top_share).astype(jnp.bfloat16)
     top_own = solve_piece(

time: 325 us -> 908 us (2.79)
  waiting for transfers between devices: 287 us -> 843 us
  other arithmetic: 6.48 us -> 21.7 us
  local copies, waits for them, and re-layouts: 4.84 us -> 16.6 us
    all_gather x0 -> x1, waiting for transfers between devices: none -> 636 us  [local(): summed_rows = jnp.sum(all_gather(top_terms, 'row'), 0)]
    psum x1 -> x0, waiting for transfers between devices: 81.3 us -> none  [local(): summed_rows = lax.psum(top_terms, 'row')]
    reduce_sum x0 -> x1, other arithmetic: none -> 15.1 us  [local(): summed_rows = jnp.sum(all_gather(top_terms, 'row'), 0)]
where the time goes in v1:
time: 908 us; the launch traced here: 907 us
  waiting for transfers between devices  843 us (93%)
  other arithmetic  21.7 us (2%)
  local copies, waits for them, and re-layouts  16.6 us (2%)
  between operations  14.6 us (2%)
  matrix products  11.4 us (1%)
    all_gather x1, waiting for transfers between devices, local(): summed_rows = jnp.sum(all_gather(top_terms, 'row'), 0)  636 us
    reduce_scatter x1, waiting for transfers between devices, local(): lax.psum_scatter(mid_terms, 'row', scatter_dimension=1, tiled=True)  90.5 us
    all_gather x1, waiting for transfers between devices, local(): lax.all_gather(mid_resid, 'row', axis=1, tiled=True)  50.7 us
    reduce_scatter x1, waiting for transfers between devices, local(): lax.psum_scatter(summed_rows, 'col', scatter_dimension=1, tiled=True)  43.3 us
    all_gather x1, waiting for transfers between devices, local(): lax.all_gather(top_resid, 'col', axis=1, tiled=True)  22.1 us
  transfers between devices with their start and end apart: 5, of which 5 were waited for; matrix products, arithmetic and copies ran while one was open for 0% of the time, Pallas kernels for 0%

profile of v1, /device:TPU:0, one launch (start us, length us, event | category | flops | bytes accessed | tf_op | source)
XLA Modules:
  0.0 907.3 jit_solution(14379753893101919449)
XLA Ops:
  7.2 0.0 copy-start
  7.2 0.0 reduce-scatter.3.cloned.1.call-start
  8.0 0.8 copy-done
  8.8 0.0 copy-start.5
  8.8 2.6 fusion.7
  11.4 0.0 copy-start.7
  11.4 1.0 copy-done.7
  12.4 0.0 copy-done.5
  12.4 1.3 fusion.4
  13.7 2.7 broadcast_select_fusion
  16.4 0.0 copy-start.4
  16.4 0.0 copy-start.6
  16.4 0.0 reduce-scatter.3.cloned.1.call-update
  16.4 0.0 all-gather.5.cloned.1.call-start
  16.4 0.9 copy-done.4
  17.3 0.2 copy.21
  17.5 0.0 copy-start.2
  17.5 90.5 %reduce-scatter.3.cloned.1.call-done = f32[2,128,512]{1,2,0:T(8,128)} async-done(((f32[2,1024,512]{1,2,0:T(8,128)}), f32[2,128,512]{1,2,0:T(8,128)}) %reduce-scatter.3.cloned.1.call-update) | async-done | bytes 524304 | tf_op jit(solution)/shard_map/reduce_scatter | solution.py:33
  107.9 1.8 subtract_convert_fusion.1
  109.7 0.0 all-gather.5.cloned.1.call-update
  109.8 0.0 all-gather.9.cloned.1.call-start
  109.8 50.7 %all-gather.5.cloned.1.call-done = bf16[2,1024,512]{1,2,0:T(8,128)(2,1)} async-done(((bf16[2,128,512]{1,2,0:T(8,128)(2,1)}), bf16[2,1024,512]{1,2,0:T(8,128)(2,1)}) %all-gather.5.cloned.1.call-update) | async-done | bytes 2097168 | tf_op jit(solution)/shard_map/all_gather | solution.py:36
  160.6 0.0 copy-done.6
  160.6 2.3 convolution_convert_fusion.1
  162.9 0.0 copy-done.2
  162.9 2.7 convolution_bitcast_fusion
  165.5 5.3 copy.23
  170.9 0.0 all-gather.9.cloned.1.call-update
  170.9 0.0 reduce-scatter.5.cloned.1.call-start
  171.0 636.0 %all-gather.9.cloned.1.call-done = f32[16,1024,512]{2,1,0:T(8,128)} async-done(((f32[2,1024,512]{2,1,0:T(8,128)}), f32[16,1024,512]{2,1,0:T(8,128)}) %all-gather.9.cloned.1.call-update) | async-done | bytes 33554448 | tf_op jit(solution)/shard_map/all_gather | solution.py:41
  806.9 15.1 %reduce_sum.9 = f32[2,1024,512]{2,1,0:T(8,128)} reduce(f32[8,2,1024,512]{3,2,1,0:T(8,128)} %bitcast.31, f32[]{:T(128)} %constant.0.clone.1), dimensions={0}, to_apply=%region_1.2 | reduce | flops 7340032 | bytes 37748740 | tf_op jit(solution)/shard_map/reduce_sum | solution.py:41
  822.0 5.4 copy.24
  827.5 0.0 copy-start.3
  827.5 0.0 reduce-scatter.5.cloned.1.call-update
  827.5 0.0 all-gather.7.cloned.1.call-start
  827.5 1.0 copy-done.3
  828.5 0.2 copy.22
  828.7 43.3 %reduce-scatter.5.cloned.1.call-done = f32[2,256,512]{1,2,0:T(8,128)} async-done(((f32[2,1024,512]{1,2,0:T(8,128)}), f32[2,256,512]{1,2,0:T(8,128)}) %reduce-scatter.5.cloned.1.call-update) | async-done | bytes 1048592 | tf_op jit(solution)/shard_map/reduce_scatter | solution.py:42
  872.0 2.1 subtract_convert_fusion
  874.1 0.0 all-gather.7.cloned.1.call-update
  874.2 0.0 copy-start.1
  874.2 0.9 copy.25
  875.0 22.1 %all-gather.7.cloned.1.call-done = bf16[2,1024,512]{1,2,0:T(8,128)(2,1)} async-done(((bf16[2,256,512]{1,2,0:T(8,128)(2,1)}), bf16[2,1024,512]{1,2,0:T(8,128)(2,1)}) %all-gather.7.cloned.1.call-update) | async-done | bytes 2097168 | tf_op jit(solution)/shard_map/all_gather | solution.py:45
  897.2 2.6 fusion.10
  899.7 1.0 copy.26
  900.7 0.0 copy-done.1
  (1 shorter events, 0.0 us)
Async XLA Ops:
  7.2 1.6 copy-start
  7.2 100.8 %reduce-scatter.3.cloned.1.call-start = ((), (), s32[]{:S(2)}) async-start(), calls=%async_computation.2 | async-start | bytes 4718592 | tf_op jit(solution)/shard_map/reduce_scatter | solution.py:33
  8.8 3.6 copy-start.5
  11.4 1.0 copy-start.7
  16.4 0.9 copy-start.4
  16.4 144.2 %copy-start.6 = (bf16[2,1024,128]{2,1,0:T(8,128)(2,1)S(1)}, bf16[2,1024,128]{2,1,0:T(8,128)(2,1)}, u32[]{:S(2)}) copy-start(bf16[2,1024,128]{2,1,0:T(8,128)(2,1)} %param.12) | copy-start | bytes 1572868
  16.4 144.2 %all-gather.5.cloned.1.call-start = ((), (), s32[]{:S(2)}) async-start(), calls=%async_computation.3 | async-start | bytes 2359296 | tf_op jit(solution)/shard_map/all_gather | solution.py:36
  17.5 145.4 %copy-start.2 = (bf16[2,1024,128]{2,1,0:T(8,128)(2,1)S(1)}, bf16[2,1024,128]{2,1,0:T(8,128)(2,1)}, u32[]{:S(2)}) copy-start(bf16[2,1024,128]{2,1,0:T(8,128)(2,1)} %param.14) | copy-start | bytes 1572868
  109.8 697.1 %all-gather.9.cloned.1.call-start = ((), (), s32[]{:S(2)}) async-start(), calls=%async_computation.6 | async-start | bytes 37748736 | tf_op jit(solution)/shard_map/all_gather | solution.py:41
  170.9 701.1 %reduce-scatter.5.cloned.1.call-start = ((), (), s32[]{:S(2)}) async-start(), calls=%async_computation.4 | async-start | bytes 5242880 | tf_op jit(solution)/shard_map/reduce_scatter | solution.py:42
  827.5 1.0 copy-start.3
  827.5 69.7 %all-gather.7.cloned.1.call-start = ((), (), s32[]{:S(2)}) async-start(), calls=%async_computation.5 | async-start | bytes 2621440 | tf_op jit(solution)/shard_map/all_gather | solution.py:45
  874.2 26.6 %copy-start.1 = (bf16[1,1024,1024]{2,1,0:T(8,128)(2,1)S(1)}, bf16[1,1024,1024]{2,1,0:T(8,128)(2,1)}, u32[]{:S(2)}) copy-start(bf16[1,1024,1024]{2,1,0:T(8,128)(2,1)} %param.9) | copy-start | bytes 6291460
Sparse Core Ops, SparseCore 0:
  16.5 91.3 reduce-scatter.2
  110.6 49.9 all-gather.4
  171.0 635.8 all-gather.8
  827.6 44.3 reduce-scatter.4
  874.3 22.8 all-gather.6
